TPU v7x, 32 devices: a whole 2x2x4 slice. The times are simulated.
32 devices in a mesh: row: 4 (over y, x), col: 8 (over z, core).
Axes of the slice: x: 2, y: 2, z: 4, core: 2. Of those that a mesh axis runs over, the one named last changes fastest.
Arguments:
- targets: float32 [2, 16384], P(None, ('row', 'col')), may hold values from 0 to 1
- sources: bfloat16 [2, 16384], P(None, 'col'), may hold values from 0 to 1
- omega: bfloat16 [256, 16384], P(None, 'col'), may hold values from -0.046875 to 0.046875
- tree_order: int32 [16384], P(('row', 'col')), may hold values from 0 to 16383, each once
- leaf_pivots: int32 [32, 128], P(('row', 'col')), may hold values from 0 to 511, all different within a row
- pivots_one: int32 [16, 128], replicated, may hold values from 0 to 255, all different within a row
- pivots_two: int32 [8, 128], replicated, may hold values from 0 to 255, all different within a row
- pivots_three: int32 [4, 128], replicated, may hold values from 0 to 255, all different within a row
Outputs:
- leaf_interp: float32 [16384, 128], P(('row', 'col'))
- level_one_interp: float32 [4096, 128], P(('row', 'col'))
- level_two_interp: float32 [2048, 128], P(('row', 'col'))
- level_three_interp: float32 [1024, 128], P(('row', 'col'))
- root_sketch: float32 [512, 256], P(('row', 'col'))
Inputs may be any that keep to these rules, and one draw needn't show every extreme that they name: tree_order names every target point once. `leaf_pivots`: each row names 128 distinct positions. `pivots_one`: each row names 128 distinct positions. `pivots_two`: each row names 128 distinct positions. `pivots_three`: each row names 128 distinct positions.
All inputs are finite; a program needn't handle non-finite values.
Results may differ from a plain program's by a relative error of at most 0.0074.
Values may be sent and summed in bfloat16 or wider, within the bound.
A program may use at most 192 MiB of HBM per device.

v0:
```python
import math

import jax
import jax.numpy as jnp
from jax import lax
from jax.sharding import PartitionSpec as P

LEAF = 512
S = 256
LEVELS = 3


RIDGE = 0.1
DELTA_SQUARED = 0.0001


def partner_2(block, axis, stride):
    count = lax.axis_size(axis)
    route = []
    for low in range(count):
        high = low | 1 << stride
        if high != low and high < count:
            route += [(low, high), (high, low)]
    return lax.ppermute(block, axis, route)


def kernel_block(points, source_pts):
    delta_x = points[0][:, None] - source_pts[0][None, :].astype(jnp.float32)
    delta_y = points[1][:, None] - source_pts[1][None, :].astype(jnp.float32)
    return (-0.5 * jnp.log(delta_x * delta_x + delta_y * delta_y + DELTA_SQUARED)).astype(
        jnp.bfloat16
    )


def select_factor(candidates, pivots):
    chosen = jnp.take(candidates, pivots, axis=0)
    gram_matrix = jnp.dot(chosen, chosen.T, precision=lax.Precision.HIGHEST)
    ridge_shift = RIDGE * (jnp.trace(gram_matrix) / chosen.shape[0] + 1e-06)
    shifted = gram_matrix + ridge_shift * jnp.eye(chosen.shape[0], dtype=gram_matrix.dtype)
    return (chosen, jnp.linalg.cholesky(shifted))


def solve_rows(chosen, factor, row_block):
    right_side = jnp.dot(chosen, row_block.T, precision=lax.Precision.HIGHEST)
    first = lax.linalg.triangular_solve(factor, right_side, left_side=True, lower=True)
    second = lax.linalg.triangular_solve(
        factor, first, left_side=True, lower=True, transpose_a=True
    )
    return second.T


def sketch_product(points, source_pts, weights):
    panel = kernel_block(points, source_pts)
    return lax.dot_general(
        panel, weights, (((1,), (1,)), ((), ())), preferred_element_type=jnp.float32
    )


def body(targets, sources, omega, tree_order, leaf_pivots, pivots_one, pivots_two, pivots_three):
    everyone = lax.all_gather(targets, ("row", "col"), axis=1, tiled=True)
    col_count = lax.axis_size("col")
    col_index = lax.axis_index("col")
    row_index = lax.axis_index("row")
    global_index = row_index * col_count + col_index
    positions = lax.all_gather(tree_order, "col", axis=0, tiled=True)
    placed = jnp.take(everyone, positions, axis=1)
    block_len = math.gcd(LEAF * lax.axis_size("col"), LEAF)
    blocks = placed.reshape(2, LEAF * lax.axis_size("col") // block_len, block_len).transpose(
        1, 0, 2
    )

    def one_block(points):
        return sketch_product(points, sources, omega)

    leaf_sketch = lax.psum_scatter(
        lax.map(one_block, blocks).reshape(LEAF * lax.axis_size("col"), S),
        "col",
        scatter_dimension=0,
        tiled=True,
    )
    chosen, factor = select_factor(leaf_sketch, leaf_pivots[0])
    results = [solve_rows(chosen, factor, leaf_sketch)]
    tables = (pivots_one, pivots_two, pivots_three)
    for section in range(LEVELS):
        partner = partner_2(chosen, "col", section)
        high_half = col_index >> section & 1 == 1
        candidates = jnp.where(
            high_half, jnp.concatenate([partner, chosen], 0), jnp.concatenate([chosen, partner], 0)
        )
        node_index = global_index >> section + 1
        node_pivots = lax.dynamic_index_in_dim(tables[section], node_index, 0, keepdims=False)
        group_size = 2 ** (section + 1)
        share_rows = candidates.shape[0] // group_size
        my_rows = lax.dynamic_slice_in_dim(
            candidates, col_index % group_size * share_rows, share_rows, 0
        )
        chosen, factor = select_factor(candidates, node_pivots)
        results.append(solve_rows(chosen, factor, my_rows))
    root_rows = chosen.shape[0] // 2**LEVELS
    root_share = lax.dynamic_slice_in_dim(chosen, col_index % 2**LEVELS * root_rows, root_rows, 0)
    return (results[0], results[1], results[2], results[3], root_share)


def solution(mesh):
    return jax.shard_map(
        body,
        mesh=mesh,
        in_specs=(
            P(None, ("row", "col")),
            P(None, "col"),
            P(None, "col"),
            P(("row", "col")),
            P(("row", "col"), None),
            P(),
            P(),
            P(),
        ),
        out_specs=(
            P(("row", "col"), None),
            P(("row", "col"), None),
            P(("row", "col"), None),
            P(("row", "col"), None),
            P(("row", "col"), None),
        ),
        check_vma=False,
    )
```

profile of v0, /device:TPU:0, one launch (start us, length us, event | category | flops | bytes accessed | tf_op | source)
XLA Modules:
  0.0 331.0 jit_solution(13750035460715798089)
XLA Ops:
  7.2 14.6 %all-gather = s32[8,1,512]{2,1,0:T(1,128)S(1)} all-gather(s32[1,1,512]{2,1,0:T(1,128)} %bitcast.123), channel_id=1, replica_groups=mesh['row'=4,'col'=8] {'col'}, dimensions={0}, use_global_device_ids=true | all-gather | bytes 18432 | tf_op jit(solution)/shard_map/all_gather | solution.py:65
  21.9 0.8 copy.23
  22.7 103.6 %all_gather.7 = f32[2,16384]{0,1:T(8,128)} all-gather(f32[2,512]{0,1:T(8,128)S(1)} %copy.23), channel_id=1, replica_groups=mesh['row'=4,'col'=8] {'row','col'}, dimensions={1}, use_global_device_ids=true | all-gather | bytes 135168 | tf_op jit(solution)/shard_map/all_gather | solution.py:60
  126.3 14.1 %gather_fusion = f32[4096,2]{1,0:T(8,128)S(1)} fusion(f32[2,16384]{0,1:T(8,128)} %all_gather.7, s32[4096]{0:T(1024)S(1)} %fusion.51), kind=kCustom, calls=%fused_computation.3 | custom fusion | bytes 81920 | tf_op jit(solution)/shard_map/jit(_take)/gather | solution.py:66
  140.5 0.6 copy.24
  141.2 18.9 %while.10 = (s32[]{:T(128)}, f32[8,512,256]{2,1,0:T(8,128)}, f32[8,2,512]{2,1,0:T(2,128)S(1)}, bf16[2,2048]{1,0:T(2,128)(2,1)S(1)}, bf16[256,2048]{1,0:T(8,128)(2,1)S(1)}, /*index=5*/s32[]{:T(128)}, s32[]{:T(128)}, s32[]{}) while((s32[]{:T(128)}, f32[8,512,256]{2,1,0:T(8,128)}, f32[8,2,512]{2,1,0:T(2,128)S(1)}, bf16[2,2048]{1,0:T(2,128)(2,1)S(1)}, ...), condition=%wide.region_1.2_spmd, body=%wide.region_0.1_spmd.sunk | while | flops 545263616 | bytes 1626729 | solution.py:76
  141.2 2.4 fusion.85
  143.6 2.4 fusion.85
  146.0 2.3 fusion.85
  148.4 2.3 fusion.85
  150.7 2.3 fusion.85
  153.1 2.3 fusion.85
  155.4 2.3 fusion.85
  157.8 2.3 fusion.85
  160.2 0.7 compare_and_fusion.3
  160.9 0.7 compare_and_fusion.2
  161.6 0.7 compare_and_fusion.1
  162.4 48.2 %reduce-scatter.2.cloned.1.call-done = f32[512,256]{1,0:T(8,128)} async-done(((f32[4096,256]{1,0:T(8,128)}), f32[512,256]{1,0:T(8,128)}) %reduce-scatter.2.cloned.1.call-update) | async-done | bytes 524304 | tf_op jit(solution)/shard_map/reduce_scatter | solution.py:75
  210.6 1.8 gather_fusion.1
  212.6 0.9 fusion.39
  214.1 0.1 copy.25
  214.2 0.1 copy.26
  214.3 11.7 %cholesky.74 = f32[128,128]{1,0:T(8,128)S(1)} custom-call(f32[128,128]{1,0:T(8,128)S(1)} %copy.26), custom_call_target="Cholesky" | custom-call | tf_op jit(solution)/shard_map/jit(cholesky)/cholesky | solution.py:40
  226.1 0.6 compare_reduce_fusion.3
  226.7 0.7 fusion.7
  227.4 9.8 %custom-call.22 = f32[1,128,128]{1,2,0:T(8,128)S(1)} custom-call(f32[1,128,128]{2,1,0:T(8,128)S(1)} %fusion.7), custom_call_target="InvertDiagBlocksLowerTriangular" | custom-call | tf_op jit(solution)/shard_map/triangular_solve | solution.py:46
  237.2 1.7 fusion.59
  238.9 0.4 fusion.28
  239.3 1.3 fusion.26
  240.6 0.8 gather_fusion.2
  241.5 0.1 collective-permute-start.1
  241.6 0.9 fusion.41
  243.2 0.1 copy.27
  243.3 0.1 copy.28
  243.4 11.9 %cholesky.85 = f32[128,128]{1,0:T(8,128)S(1)} custom-call(f32[128,128]{1,0:T(8,128)S(1)} %copy.28), custom_call_target="Cholesky" | custom-call | tf_op jit(solution)/shard_map/jit(cholesky)/cholesky | solution.py:40
  255.3 0.6 compare_reduce_fusion.2
  255.9 0.7 fusion.8
  256.6 9.8 %custom-call.23 = f32[1,128,128]{1,2,0:T(8,128)S(1)} custom-call(f32[1,128,128]{2,1,0:T(8,128)S(1)} %fusion.8), custom_call_target="InvertDiagBlocksLowerTriangular" | custom-call | tf_op jit(solution)/shard_map/triangular_solve | solution.py:46
  266.4 0.3 fusion.5
  266.7 0.3 fusion.23
  267.0 0.9 fusion.21
  267.9 0.8 gather_fusion.3
  268.8 1.5 collective-permute-start.2
  270.3 0.9 fusion.43
  271.9 0.1 copy.30
  272.0 11.7 %cholesky.96 = f32[128,128]{1,0:T(8,128)S(1)} custom-call(f32[128,128]{1,0:T(8,128)S(1)} %copy.30), custom_call_target="Cholesky" | custom-call | tf_op jit(solution)/shard_map/jit(cholesky)/cholesky | solution.py:40
  283.8 0.6 compare_reduce_fusion.1
  284.4 0.7 fusion.9
  285.1 9.8 %custom-call.24 = f32[1,128,128]{1,2,0:T(8,128)S(1)} custom-call(f32[1,128,128]{2,1,0:T(8,128)S(1)} %fusion.9), custom_call_target="InvertDiagBlocksLowerTriangular" | custom-call | tf_op jit(solution)/shard_map/triangular_solve | solution.py:46
  294.9 0.3 fusion.47
  295.2 0.3 fusion.18
  295.5 0.9 fusion.16
  296.4 0.8 gather_fusion.4
  297.2 0.9 fusion.45
  298.8 0.1 copy.31
  298.9 0.1 copy.32
  299.0 12.0 %cholesky.107 = f32[128,128]{1,0:T(8,128)S(1)} custom-call(f32[128,128]{1,0:T(8,128)S(1)} %copy.32), custom_call_target="Cholesky" | custom-call | tf_op jit(solution)/shard_map/jit(cholesky)/cholesky | solution.py:40
  311.0 0.6 compare_reduce_fusion
  311.6 0.7 fusion.10
  312.3 9.8 %custom-call.25 = f32[1,128,128]{1,2,0:T(8,128)S(1)} custom-call(f32[1,128,128]{2,1,0:T(8,128)S(1)} %fusion.10), custom_call_target="InvertDiagBlocksLowerTriangular" | custom-call | tf_op jit(solution)/shard_map/triangular_solve | solution.py:46
  322.1 0.3 fusion.49
  322.4 0.3 fusion.13
  322.7 0.9 fusion.11
  323.5 0.6 constant_dynamic-slice_fusion.2
  (59 shorter events, 1.2 us)
Async XLA Ops:
  7.2 203.4 %reduce-scatter.2.cloned.1.call-start = ((), (), s32[]{:S(2)}) async-start(), calls=%async_computation.1 | async-start | bytes 4718592 | tf_op jit(solution)/shard_map/reduce_scatter | solution.py:75
  22.7 118.5 %copy-start = (bf16[2,2048]{1,0:T(2,128)(2,1)S(1)}, bf16[2,2048]{1,0:T(2,128)(2,1)}, u32[]{:S(2)}) copy-start(bf16[2,2048]{1,0:T(2,128)(2,1)} %param.14) | copy-start | bytes 24580
  22.7 118.5 %copy-start.1 = (bf16[256,2048]{1,0:T(8,128)(2,1)S(1)}, bf16[256,2048]{1,0:T(8,128)(2,1)}, u32[]{:S(2)}) copy-start(bf16[256,2048]{1,0:T(8,128)(2,1)} %param.15) | copy-start | bytes 3145732
  160.1 2.2 copy-start.2
  212.5 28.1 %collective-permute-start = (f32[128,256]{1,0:T(8,128)S(1)}, f32[128,256]{1,0:T(8,128)S(1)}, u32[]{:S(2)}, u32[]{:S(2)}) collective-permute-start(f32[128,256]{1,0:T(8,128)S(1)} %broadcast_select_fusion.3), channel_id=1, source_target_pairs={{0,1},{1,0},{2,3},{3,2},{4,5},{5,4},{6,7},{7,6},{8,9},{9,8},{10,11... | collective-permute-start | bytes 393224 | tf_op jit(solution)/shard_map/ppermute | solution.py:24
  241.5 26.4 %collective-permute-start.1 = (f32[128,256]{1,0:T(8,128)S(1)}, f32[128,256]{1,0:T(8,128)S(1)}, u32[]{:S(2)}, u32[]{:S(2)}) collective-permute-start(f32[128,256]{1,0:T(8,128)S(1)} %broadcast_select_fusion.2), channel_id=1, source_target_pairs={{0,2},{2,0},{1,3},{3,1},{4,6},{6,4},{5,7},{7,5},{8,10},{10,8},{9,1... | collective-permute-start | bytes 393224 | tf_op jit(solution)/shard_map/ppermute | solution.py:24
  268.8 27.6 %collective-permute-start.2 = (f32[128,256]{1,0:T(8,128)S(1)}, f32[128,256]{1,0:T(8,128)S(1)}, u32[]{:S(2)}, u32[]{:S(2)}) collective-permute-start(f32[128,256]{1,0:T(8,128)S(1)} %broadcast_select_fusion.1), channel_id=1, source_target_pairs={{0,4},{4,0},{1,5},{5,1},{2,6},{6,2},{3,7},{7,3},{8,12},{12,8},{9,1... | collective-permute-start | bytes 393224 | tf_op jit(solution)/shard_map/ppermute | solution.py:24
Sparse Core Ops, SparseCore 0:
  160.3 50.2 reduce-scatter.1
where the time goes:
time: 331 us
  blocking collectives  118 us (36%)
  other arithmetic  94.6 us (29%)
  waiting for transfers between devices  48.2 us (15%)
  matrix products  29.9 us (9%)
  local copies, waits for them, and re-layouts  21.1 us (6%)
  between operations  17.1 us (5%)
    all_gather x1, blocking collectives, body(): everyone = lax.all_gather(targets, ('row', 'col'), axis=1, tiled=True)  104 us
    another operation x12, other arithmetic, select_factor(): return (chosen, jnp.linalg.cholesky(shifted))  50 us
    reduce_scatter x1, waiting for transfers between devices, body(): lax.psum_scatter(lax.map(one_block, blocks).reshape(LEAF * lax.axis_size(...  48.2 us
    another operation x8, other arithmetic, solve_rows(): lax.linalg.triangular_solve(factor, first, left_side=True, lower=True, tr...  41.9 us
    dot_general x8, matrix products, sketch_product(): lax.dot_general(panel, weights, (((1,), (1,)), ((), ())), preferred_eleme...  18.7 us
    gather x2, local copies, waits for them, and re-layouts, body(): placed = jnp.take(everyone, positions, axis=1)  14.8 us
    all_gather x1, blocking collectives, body(): positions = lax.all_gather(tree_order, 'col', axis=0, tiled=True)  14.6 us
  transfers between devices with their start and end apart: 4, of which 1 were waited for; matrix products, arithmetic and copies ran while one was open for 24% of the time, Pallas kernels for 0%

commit v1 on v0

v1 whole, which is shorter than its diff:
```python
import functools

import jax
import jax.numpy as jnp
from jax import lax
from jax.experimental import pallas as pl
from jax.experimental.pallas import tpu as pltpu
from jax.sharding import PartitionSpec as P

RIDGE = 0.1
DELTA_SQUARED = 0.0001
LEVELS = 3
LANES = 128
CHUNK = 512
MESH = pl.DeviceIdType.MESH
HIGHEST = lax.Precision.HIGHEST
F32 = jnp.float32
BF16 = jnp.bfloat16


def split3(x):
    a = x.astype(BF16)
    r = x - a.astype(F32)
    b = r.astype(BF16)
    c = (r - b.astype(F32)).astype(BF16)
    return a, b, c


def pick_columns(pieces, pivots):
    m = pieces[0].shape[1]
    hot = (
        lax.broadcasted_iota(jnp.int32, (m, pivots.shape[1]), 0) == pivots
    ).astype(F32).astype(BF16)
    out = None
    for piece in pieces:
        term = jnp.dot(piece, hot, preferred_element_type=F32)
        out = term if out is None else out + term
    return out


def sketch_kernel(
    rows, cols,
    tgt_ref, src_ref, om_ref, ord_ref, leaf_ref, p1_ref, p2_ref, p3_ref,
    sk_ref, ch_ref,
    every, orders, table, acc, part_out, part_in, z_out, z_in, ex_out, ex_in,
    tgt_send, tgt_recv, ord_send, ord_recv, part_send, part_recv, z_send, z_recv, ex_send, ex_recv,
):
    n = rows * cols
    zs = cols // 2
    row = lax.axis_index("row")
    col = lax.axis_index("col")
    me = row * cols + col
    z = col // 2
    core = col % 2
    partner = z * 2 + (1 - core)
    length = ord_ref.shape[1]
    per = tgt_ref.shape[0]

    barrier = pltpu.get_barrier_semaphore()

    def greet(i, carry):
        other = lax.rem(me + i, n)
        pl.semaphore_signal(
            barrier, inc=1, device_id=(other // cols, other % cols), device_id_type=MESH
        )
        return carry

    lax.fori_loop(1, n, greet, 0)
    pl.semaphore_wait(barrier, n - 1)

    def tgt_copy(i):
        other = lax.rem(me + i, n)
        return pltpu.make_async_remote_copy(
            src_ref=tgt_ref, dst_ref=every.at[me],
            send_sem=tgt_send.at[i], recv_sem=tgt_recv.at[i],
            device_id=(other // cols, other % cols), device_id_type=MESH,
        )

    def ord_copy(i):
        other = lax.rem(col + i, cols)
        return pltpu.make_async_remote_copy(
            src_ref=ord_ref, dst_ref=orders.at[col],
            send_sem=ord_send.at[i], recv_sem=ord_recv.at[i],
            device_id=(row, other), device_id_type=MESH,
        )

    def start(copy):
        def go(i, carry):
            copy(i).start()
            return carry
        return go

    def finish(copy):
        def go(i, carry):
            copy(i).wait()
            return carry
        return go

    lax.fori_loop(1, n, start(tgt_copy), 0)
    lax.fori_loop(1, cols, start(ord_copy), 0)
    every[me] = tgt_ref[...]
    orders[col] = ord_ref[...]
    lax.fori_loop(1, n, finish(tgt_copy), 0)
    lax.fori_loop(1, cols, finish(ord_copy), 0)

    flat = every[...].reshape(n * per, LANES).T
    for i, piece in enumerate(split3(flat)):
        table[i] = piece

    half = per // 2

    def points_of(leaf):
        order = orders[leaf]
        owner_row = order // (half * LANES) * per + order // LANES % half
        lane = order % LANES
        rows_iota = lax.broadcasted_iota(jnp.int32, (n * per, length), 0)
        lane_iota = lax.broadcasted_iota(jnp.int32, (LANES, length), 0)
        out = []
        for c in range(2):
            hot = (rows_iota == owner_row + c * half).astype(F32).astype(BF16)
            got = jnp.dot(table[0], hot, preferred_element_type=F32)
            got += jnp.dot(table[1], hot, preferred_element_type=F32)
            got += jnp.dot(table[2], hot, preferred_element_type=F32)
            out.append(jnp.sum(jnp.where(lane_iota == lane, got, 0.0), axis=0, keepdims=True))
        return out

    sources = src_ref.shape[0]

    def block(leaf):
        px, py = points_of(leaf)
        acc[...] = jnp.zeros_like(acc)

        def chunk(i, carry):
            at = pl.multiple_of(i * CHUNK, CHUNK)
            s = src_ref[pl.ds(at, CHUNK), :]
            dx = px - s[:, 0:1]
            dy = py - s[:, 1:2]
            panel = (-0.5 * jnp.log(dx * dx + dy * dy + DELTA_SQUARED)).astype(BF16)
            acc[...] += jnp.dot(
                om_ref[:, pl.ds(at, CHUNK)], panel, preferred_element_type=F32
            )
            return carry

        lax.fori_loop(0, sources // CHUNK, chunk, 0)

    def part_copy(k):
        return pltpu.make_async_remote_copy(
            src_ref=part_out.at[k], dst_ref=part_in.at[k],
            send_sem=part_send.at[k], recv_sem=part_recv.at[k],
            device_id=(row, partner), device_id_type=MESH,
        )

    def z_copy(k):
        to = lax.rem(z + k, zs)
        return pltpu.make_async_remote_copy(
            src_ref=z_out.at[k], dst_ref=z_in.at[k],
            send_sem=z_send.at[k], recv_sem=z_recv.at[k],
            device_id=(row, to * 2 + core), device_id_type=MESH,
        )

    def both(k):
        to = lax.rem(z + k, zs)
        block(to * 2 + (1 - core))
        part_out[k] = acc[...].astype(BF16)
        part_copy(k).start()
        block(to * 2 + core)
        part_copy(k).wait()

    def step(k, carry):
        both(k)
        z_out[k] = (acc[...] + part_in[k].astype(F32)).astype(BF16)
        z_copy(k).start()
        return carry

    lax.fori_loop(1, zs, step, 0)
    both(0)
    acc[...] += part_in[0].astype(F32)

    def collect(k, carry):
        z_copy(k).wait()
        acc[...] += z_in[k].astype(F32)
        return carry

    lax.fori_loop(1, zs, collect, 0)

    sk_ref[...] = acc[...]
    chosen = pick_columns(split3(acc[...]), leaf_ref[...])
    ch_ref[0] = chosen
    for s, p_ref in enumerate((p1_ref, p2_ref, p3_ref)):
        bit = col // 2**s % 2
        other = col + (1 - 2 * bit) * 2**s
        ex_out[s] = chosen
        copy = pltpu.make_async_remote_copy(
            src_ref=ex_out.at[s], dst_ref=ex_in.at[s],
            send_sem=ex_send.at[s], recv_sem=ex_recv.at[s],
            device_id=(row, other), device_id_type=MESH,
        )
        copy.start()
        copy.wait()
        theirs = ex_in[s]
        high = bit == 1
        low_part = jnp.where(high, theirs, chosen)
        high_part = jnp.where(high, chosen, theirs)
        cand = jnp.concatenate([low_part, high_part], axis=1)
        chosen = pick_columns(split3(cand), p_ref[pl.ds(me // 2 ** (s + 1), 1), :])
        ch_ref[s + 1] = chosen


def contract0(a, b):
    return lax.dot_general(
        a, b, (((0,), (0,)), ((), ())), precision=HIGHEST, preferred_element_type=F32
    )


def solve_kernel(sk_ref, ch_ref, o0, o1, o2, o3, root, a_ref, r_ref, t_ref):
    col = lax.axis_index("col")
    k = ch_ref.shape[2]
    levels = ch_ref.shape[0]
    lane2 = lax.broadcasted_iota(jnp.int32, (k, k), 1)
    sub2 = lax.broadcasted_iota(jnp.int32, (k, k), 0)
    for m in range(levels):
        gram = contract0(ch_ref[m], ch_ref[m])
        eye = lane2 == sub2
        trace = jnp.sum(jnp.where(eye, gram, 0.0))
        shift = RIDGE * (trace / k + 1e-06)
        a_ref[m] = gram + jnp.where(eye, shift, 0.0)

    lane1 = lax.broadcasted_iota(jnp.int32, (1, k), 1)

    def step(i, carry):
        here = lane2 == i
        here1 = lane1 == i
        for m in range(levels):
            a = a_ref[m]
            r = a_ref[m, pl.ds(i, 1), :]
            c = jnp.sum(jnp.where(here, a, 0.0), axis=1, keepdims=True)
            p = 1.0 / jnp.sum(jnp.where(here1, r, 0.0), axis=1, keepdims=True)
            rp = jnp.where(here1, p, r * p)
            a_ref[m] = jnp.where(here, 0.0, a) - c * rp
            a_ref[m, pl.ds(i, 1), :] = rp
        return carry

    lax.fori_loop(0, k, step, 0)
    right = contract0(sk_ref[...], ch_ref[0])
    o0[...] = jnp.dot(right, a_ref[0], precision=HIGHEST, preferred_element_type=F32)
    for s, o in enumerate((o1, o2, o3)):
        r_ref[...] = contract0(ch_ref[s], ch_ref[s + 1])
        size = o.shape[0]
        at = pl.multiple_of(col % 2**s * size, size)
        o[...] = jnp.dot(
            r_ref[pl.ds(at, size), :], a_ref[s + 1], precision=HIGHEST,
            preferred_element_type=F32,
        )
    t_ref[...] = ch_ref[levels - 1].T
    size = root.shape[0]
    root[...] = t_ref[pl.ds(pl.multiple_of(col % 2**LEVELS * size, size), size), :]


def body(rows, cols, targets, sources, omega, tree_order, leaf_pivots, p1, p2, p3):
    n = rows * cols
    zs = cols // 2
    leaf = tree_order.shape[0]
    width = omega.shape[0]
    k = leaf_pivots.shape[1]
    per = targets.size // LANES
    vmem = pl.BlockSpec(memory_space=pltpu.VMEM)
    dma = lambda *d: pltpu.SemaphoreType.DMA(d)
    sketch, chosen = pl.pallas_call(
        functools.partial(sketch_kernel, rows, cols),
        out_shape=(
            jax.ShapeDtypeStruct((width, leaf), F32),
            jax.ShapeDtypeStruct((LEVELS + 1, width, k), F32),
        ),
        in_specs=[vmem] * 8,
        out_specs=(vmem, vmem),
        scratch_shapes=[
            pltpu.VMEM((n, per, LANES), F32),
            pltpu.VMEM((cols, 1, leaf), jnp.int32),
            pltpu.VMEM((3, LANES, n * per), BF16),
            pltpu.VMEM((width, leaf), F32),
            pltpu.VMEM((zs, width, leaf), BF16),
            pltpu.VMEM((zs, width, leaf), BF16),
            pltpu.VMEM((zs, width, leaf), BF16),
            pltpu.VMEM((zs, width, leaf), BF16),
            pltpu.VMEM((LEVELS, width, k), F32),
            pltpu.VMEM((LEVELS, width, k), F32),
            dma(n), dma(n), dma(cols), dma(cols), dma(zs), dma(zs), dma(zs), dma(zs),
            dma(LEVELS), dma(LEVELS),
        ],
        compiler_params=pltpu.CompilerParams(
            collective_id=0, has_side_effects=True, vmem_limit_bytes=48 << 20
        ),
    )(
        targets.reshape(per, LANES),
        sources.astype(F32).T,
        omega,
        tree_order.reshape(1, leaf),
        leaf_pivots,
        p1, p2, p3,
    )
    out_rows = [leaf] + [k // 2**s for s in range(LEVELS)]
    return pl.pallas_call(
        solve_kernel,
        out_shape=tuple(jax.ShapeDtypeStruct((r, k), F32) for r in out_rows)
        + (jax.ShapeDtypeStruct((k // 2**LEVELS, width), F32),),
        in_specs=[vmem, vmem],
        out_specs=(vmem,) * (len(out_rows) + 1),
        scratch_shapes=[
            pltpu.VMEM((LEVELS + 1, k, k), F32),
            pltpu.VMEM((k, k), F32),
            pltpu.VMEM((k, width), F32),
        ],
        compiler_params=pltpu.CompilerParams(vmem_limit_bytes=32 << 20),
    )(sketch, chosen)


def solution(mesh):
    both = P(("row", "col"), None)
    return jax.shard_map(
        functools.partial(body, mesh.shape["row"], mesh.shape["col"]),
        mesh=mesh,
        in_specs=(
            P(None, ("row", "col")),
            P(None, "col"),
            P(None, "col"),
            P(("row", "col")),
            both,
            P(),
            P(),
            P(),
        ),
        out_specs=(both,) * 5,
        check_vma=False,
    )
```

time: 331 us -> 115 us (0.35)
  blocking collectives: 118 us -> 0 us
  Pallas kernels: 0 us -> 111 us
  other arithmetic: 94.6 us -> 0 us
  waiting for transfers between devices: 48.2 us -> 0 us
  matrix products: 29.9 us -> 0 us
  local copies, waits for them, and re-layouts: 21.1 us -> 2.4 us
  between operations: 17.1 us -> 0.71 us
    all_gather x2 -> x0, blocking collectives: 118 us -> none  [the longest x1 104 us: body(): everyone = lax.all_gather(targets, ('row', 'col'), axis=1, tiled=True)]
    pallas_call x0 -> x2, Pallas kernels: none -> 111 us  [the longest x1 58 us: body(): pl.pallas_call(functools.partial(sketch_kernel, rows, cols), out_shape=(j...]
    another operation x20 -> x0, other arithmetic: 91.8 us -> none  [the longest x12 50 us: select_factor(): return (chosen, jnp.linalg.cholesky(shifted))]
    reduce_scatter x1 -> x0, waiting for transfers between devices: 48.2 us -> none  [body(): lax.psum_scatter(lax.map(one_block, blocks).reshape(LEAF * lax.axis_size(...]
    dot_general x16 -> x0, matrix products: 24.7 us -> none  [the longest x8 18.7 us: sketch_product(): lax.dot_general(panel, weights, (((1,), (1,)), ((), ())), preferred_eleme...]
    gather x6 -> x0, local copies, waits for them, and re-layouts: 18.8 us -> none  [the longest x2 14.8 us: body(): placed = jnp.take(everyone, positions, axis=1)]
    another operation x8 -> x0, matrix products: 5.24 us -> none  [the longest x4 3.97 us: solve_rows(): lax.linalg.triangular_solve(factor, first, left_side=True, lower=True, tr...]
  transfers between devices with their start and end apart: 4 -> 0, of which waited for: 1 -> 0; matrix products, arithmetic and copies ran while one was open for 24% -> 0% of each run, Pallas kernels for 0% -> 0%
where the time goes in v1:
time: 115 us; the launch traced here: 114 us
  Pallas kernels  111 us (97%)
  local copies, waits for them, and re-layouts  2.4 us (2%)
    pallas_call x1, Pallas kernels, body(): pl.pallas_call(functools.partial(sketch_kernel, rows, cols), out_shape=(j...  58 us
    pallas_call x1, Pallas kernels, body(): pl.pallas_call(solve_kernel, out_shape=tuple((jax.ShapeDtypeStruct((r, k)...  53.4 us

profile of v1, /device:TPU:0, one launch (start us, length us, event | category | flops | bytes accessed | tf_op | source)
XLA Modules:
  0.0 114.5 jit_solution(1541134153242224850)
XLA Ops:
  0.6 0.0 copy-start
  0.6 0.8 reshape.16.tgt_ref
  1.4 0.0 copy-start.1
  1.4 0.0 copy-start.2
  1.4 0.0 copy-start.3
  1.4 0.0 copy-start.4
  1.4 1.0 copy.13
  2.4 0.0 copy-start.5
  2.5 0.0 copy-done
  2.5 0.0 copy-done.1
  2.5 0.0 copy-done.2
  2.5 0.0 copy-done.3
  2.5 0.0 copy-done.4
  2.5 0.6 copy-done.5
  3.1 58.0 %shard_map.119 = (f32[256,512]{1,0:T(8,128)S(1)}, f32[4,256,128]{2,1,0:T(8,128)S(1)}) custom-call(f32[8,128]{1,0:T(8,128)S(1)} %reshape.16.tgt_ref, f32[2048,2]{1,0:T(8,128)S(1)} %bitcast.2, bf16[256,2048]{1,0:T(8,128)(2,1)S(1)} %copy-done, s32[1,512]{1,0:T(1,128)S(1)} %bitcast.3, s32[1,128]{1,0:T(1,128)S(1)} %copy-done.5, s32[16,128]{1,0:T(8,128)S(1)} %copy-done.1, ...), custom_call_target="tpu_custom_call" | custom-call | tf_op jit(solution)/shard_map/pallas_call | solution.py:268
  61.1 53.4 %shard_map.120 = (f32[512,128]{1,0:T(8,128)}, f32[128,128]{1,0:T(8,128)}, f32[64,128]{1,0:T(8,128)}, f32[32,128]{1,0:T(8,128)}, f32[16,256]{1,0:T(8,128)}) custom-call(f32[256,512]{1,0:T(8,128)S(1)} %get-tuple-element.7.sk_ref, f32[4,256,128]{2,1,0:T(8,128)S(1)} %get-tuple-element.8.ch_ref), custom_call_target="tpu_custom_call" | custom-call | tf_op jit(solution)/shard_map/pallas_call | solution.py:302
Async XLA Ops:
  0.6 1.8 %copy-start = (bf16[256,2048]{1,0:T(8,128)(2,1)S(1)}, bf16[256,2048]{1,0:T(8,128)(2,1)}, u32[]{:S(2)}) copy-start(bf16[256,2048]{1,0:T(8,128)(2,1)} %om_ref.1) | copy-start | bytes 3145732
  1.4 1.0 copy-start.1
  1.4 1.1 copy-start.2
  1.4 1.1 copy-start.3
  1.4 1.1 copy-start.4
  2.4 0.7 copy-start.5

commit v2 on v1

--- a/solution.py
+++ b/solution.py
@@ -11,7 +11,8 @@
 DELTA_SQUARED = 0.0001
 LEVELS = 3
 LANES = 128
-CHUNK = 512
+CHUNK = 256
+LN2 = 0.6931471805599453
 MESH = pl.DeviceIdType.MESH
 HIGHEST = lax.Precision.HIGHEST
 F32 = jnp.float32
@@ -42,7 +43,7 @@
     rows, cols,
     tgt_ref, src_ref, om_ref, ord_ref, leaf_ref, p1_ref, p2_ref, p3_ref,
     sk_ref, ch_ref,
-    every, orders, table, acc, part_out, part_in, z_out, z_in, ex_out, ex_in,
+    every, orders, table, src_col, acc, part_out, part_in, z_out, z_in, ex_out, ex_in,
     tgt_send, tgt_recv, ord_send, ord_recv, part_send, part_recv, z_send, z_recv, ex_send, ex_recv,
 ):
     n = rows * cols
@@ -54,7 +55,8 @@
     core = col % 2
     partner = z * 2 + (1 - core)
     length = ord_ref.shape[1]
-    per = tgt_ref.shape[0]
+    local = tgt_ref.shape[1]
+    per = 2 * local // LANES
 
     barrier = pltpu.get_barrier_semaphore()
 
@@ -100,48 +102,52 @@
     lax.fori_loop(1, cols, start(ord_copy), 0)
     every[me] = tgt_ref[...]
     orders[col] = ord_ref[...]
+    wide = src_ref[...].astype(F32)
+    src_col[...] = jnp.concatenate([wide, jnp.zeros((6, wide.shape[1]), F32)], axis=0).T
     lax.fori_loop(1, n, finish(tgt_copy), 0)
     lax.fori_loop(1, cols, finish(ord_copy), 0)
 
-    flat = every[...].reshape(n * per, LANES).T
+    flat = jnp.concatenate(
+        [
+            every[:, c, a * LANES : (a + 1) * LANES]
+            for a in range(local // LANES)
+            for c in range(2)
+        ],
+        axis=0,
+    ).T
     for i, piece in enumerate(split3(flat)):
         table[i] = piece
 
-    half = per // 2
-
     def points_of(leaf):
         order = orders[leaf]
-        owner_row = order // (half * LANES) * per + order // LANES % half
+        owner_row = order // LANES % (local // LANES) * (2 * n) + order // local
         lane = order % LANES
         rows_iota = lax.broadcasted_iota(jnp.int32, (n * per, length), 0)
         lane_iota = lax.broadcasted_iota(jnp.int32, (LANES, length), 0)
         out = []
         for c in range(2):
-            hot = (rows_iota == owner_row + c * half).astype(F32).astype(BF16)
+            hot = (rows_iota == owner_row + c * n).astype(F32).astype(BF16)
             got = jnp.dot(table[0], hot, preferred_element_type=F32)
             got += jnp.dot(table[1], hot, preferred_element_type=F32)
             got += jnp.dot(table[2], hot, preferred_element_type=F32)
             out.append(jnp.sum(jnp.where(lane_iota == lane, got, 0.0), axis=0, keepdims=True))
         return out
 
-    sources = src_ref.shape[0]
+    sources = src_ref.shape[1]
 
     def block(leaf):
         px, py = points_of(leaf)
-        acc[...] = jnp.zeros_like(acc)
-
-        def chunk(i, carry):
-            at = pl.multiple_of(i * CHUNK, CHUNK)
-            s = src_ref[pl.ds(at, CHUNK), :]
+        total = None
+        for at in range(0, sources, CHUNK):
+            s = src_col[at : at + CHUNK, :]
             dx = px - s[:, 0:1]
             dy = py - s[:, 1:2]
-            panel = (-0.5 * jnp.log(dx * dx + dy * dy + DELTA_SQUARED)).astype(BF16)
-            acc[...] += jnp.dot(
-                om_ref[:, pl.ds(at, CHUNK)], panel, preferred_element_type=F32
+            panel = (-0.5 * LN2) * jnp.log2(dx * dx + dy * dy + DELTA_SQUARED)
+            term = jnp.dot(
+                om_ref[:, at : at + CHUNK], panel.astype(BF16), preferred_element_type=F32
             )
-            return carry
-
-        lax.fori_loop(0, sources // CHUNK, chunk, 0)
+            total = term if total is None else total + term
+        acc[...] = total
 
     def part_copy(k):
         return pltpu.make_async_remote_copy(
@@ -212,45 +218,61 @@
     )
 
 
-def solve_kernel(sk_ref, ch_ref, o0, o1, o2, o3, root, a_ref, r_ref, t_ref):
+def halves(x):
+    h = x.astype(BF16)
+    return h, (x - h.astype(F32)).astype(BF16)
+
+
+def product3(a, b):
+    ah, al = halves(a)
+    bh, bl = halves(b)
+    dot = functools.partial(jnp.dot, preferred_element_type=F32)
+    return dot(ah, bh) + (dot(ah, bl) + dot(al, bh))
+
+
+def product6(a, b):
+    return jnp.dot(a, b, precision=HIGHEST, preferred_element_type=F32)
+
+
+def shifted_inverses(grams):
+    k = grams[0].shape[0]
+    eye = lax.broadcasted_iota(jnp.int32, (k, k), 0) == lax.broadcasted_iota(
+        jnp.int32, (k, k), 1
+    )
+    one = jnp.where(eye, 1.0, 0.0)
+    low = 1.0 / (k / RIDGE + 1.0)
+    gap = (1.0 - low) / (1.0 + low)
+    first = 2.0 / (1.0 + low)
+    tops, mats = [], []
+    for gram in grams:
+        trace = jnp.sum(jnp.where(eye, gram, 0.0), axis=(0, 1), keepdims=True)
+        shift = RIDGE * (trace / k + 1e-06)
+        tops.append(trace + shift)
+        mats.append((gram + shift * one) / (trace + shift))
+    scale = 2.0 / (2.0 - gap * gap)
+    xs = [scale * (2.0 * first * one - first * first * m) for m in mats]
+    gap = gap * gap / (2.0 - gap * gap)
+    scales = []
+    while gap > 1e-9:
+        scales.append(2.0 / (2.0 - gap * gap))
+        gap = gap * gap / (2.0 - gap * gap)
+    for i, scale in enumerate(scales):
+        product = product6 if i >= len(scales) - 2 else product3
+        ys = [scale * (2.0 * one - product(m, x)) for m, x in zip(mats, xs)]
+        xs = [product(x, y) for x, y in zip(xs, ys)]
+    return [x / t for x, t in zip(xs, tops)]
+
+
+def solve_kernel(sk_ref, ch_ref, o0, o1, o2, o3, root, r_ref, t_ref):
     col = lax.axis_index("col")
-    k = ch_ref.shape[2]
     levels = ch_ref.shape[0]
-    lane2 = lax.broadcasted_iota(jnp.int32, (k, k), 1)
-    sub2 = lax.broadcasted_iota(jnp.int32, (k, k), 0)
-    for m in range(levels):
-        gram = contract0(ch_ref[m], ch_ref[m])
-        eye = lane2 == sub2
-        trace = jnp.sum(jnp.where(eye, gram, 0.0))
-        shift = RIDGE * (trace / k + 1e-06)
-        a_ref[m] = gram + jnp.where(eye, shift, 0.0)
-
-    lane1 = lax.broadcasted_iota(jnp.int32, (1, k), 1)
-
-    def step(i, carry):
-        here = lane2 == i
-        here1 = lane1 == i
-        for m in range(levels):
-            a = a_ref[m]
-            r = a_ref[m, pl.ds(i, 1), :]
-            c = jnp.sum(jnp.where(here, a, 0.0), axis=1, keepdims=True)
-            p = 1.0 / jnp.sum(jnp.where(here1, r, 0.0), axis=1, keepdims=True)
-            rp = jnp.where(here1, p, r * p)
-            a_ref[m] = jnp.where(here, 0.0, a) - c * rp
-            a_ref[m, pl.ds(i, 1), :] = rp
-        return carry
-
-    lax.fori_loop(0, k, step, 0)
-    right = contract0(sk_ref[...], ch_ref[0])
-    o0[...] = jnp.dot(right, a_ref[0], precision=HIGHEST, preferred_element_type=F32)
+    inverse = shifted_inverses([contract0(ch_ref[m], ch_ref[m]) for m in range(levels)])
+    o0[...] = product6(contract0(sk_ref[...], ch_ref[0]), inverse[0])
     for s, o in enumerate((o1, o2, o3)):
         r_ref[...] = contract0(ch_ref[s], ch_ref[s + 1])
         size = o.shape[0]
         at = pl.multiple_of(col % 2**s * size, size)
-        o[...] = jnp.dot(
-            r_ref[pl.ds(at, size), :], a_ref[s + 1], precision=HIGHEST,
-            preferred_element_type=F32,
-        )
+        o[...] = product6(r_ref[pl.ds(at, size), :], inverse[s + 1])
     t_ref[...] = ch_ref[levels - 1].T
     size = root.shape[0]
     root[...] = t_ref[pl.ds(pl.multiple_of(col % 2**LEVELS * size, size), size), :]
@@ -274,9 +296,10 @@
         in_specs=[vmem] * 8,
         out_specs=(vmem, vmem),
         scratch_shapes=[
-            pltpu.VMEM((n, per, LANES), F32),
+            pltpu.VMEM((n, 2, leaf), F32),
             pltpu.VMEM((cols, 1, leaf), jnp.int32),
             pltpu.VMEM((3, LANES, n * per), BF16),
+            pltpu.VMEM((sources.shape[1], 8), F32),
             pltpu.VMEM((width, leaf), F32),
             pltpu.VMEM((zs, width, leaf), BF16),
             pltpu.VMEM((zs, width, leaf), BF16),
@@ -291,8 +314,8 @@
             collective_id=0, has_side_effects=True, vmem_limit_bytes=48 << 20
         ),
     )(
-        targets.reshape(per, LANES),
-        sources.astype(F32).T,
+        targets,
+        sources,
         omega,
         tree_order.reshape(1, leaf),
         leaf_pivots,
@@ -306,7 +329,6 @@
         in_specs=[vmem, vmem],
         out_specs=(vmem,) * (len(out_rows) + 1),
         scratch_shapes=[
-            pltpu.VMEM((LEVELS + 1, k, k), F32),
             pltpu.VMEM((k, k), F32),
             pltpu.VMEM((k, width), F32),
         ],

time: 115 us -> 70.6 us (0.61)
  Pallas kernels: 111 us -> 63.6 us
  local copies, waits for them, and re-layouts: 2.4 us -> 6 us
    pallas_call x1, Pallas kernels: 53.4 us -> 6.74 us  [body(): pl.pallas_call(solve_kernel, out_shape=tuple((jax.ShapeDtypeStruct((r, k)...]
    unnamed x12 -> x16, local copies, waits for them, and re-layouts: 0.62 us -> 6 us
where the time goes in v2:
time: 70.6 us; the launch traced here: 70.3 us
  Pallas kernels  63.6 us (90%)
  local copies, waits for them, and re-layouts  6 us (8%)
    pallas_call x1, Pallas kernels, body(): pl.pallas_call(functools.partial(sketch_kernel, rows, cols), out_shape=(j...  56.9 us
    pallas_call x1, Pallas kernels, body(): pl.pallas_call(solve_kernel, out_shape=tuple((jax.ShapeDtypeStruct((r, k)...  6.74 us
    unnamed x16, local copies, waits for them, and re-layouts  6 us

profile of v2, /device:TPU:0, one launch (start us, length us, event | category | flops | bytes accessed | tf_op | source)
XLA Modules:
  0.0 70.3 jit_solution(9709130351339590013)
XLA Ops:
  0.6 0.0 copy-start.7
  0.6 0.6 copy-done.7
  1.3 0.0 copy-start
  1.3 1.2 %copy-done = bf16[256,2048]{1,0:T(8,128)(2,1)S(1)} copy-done((bf16[256,2048]{1,0:T(8,128)(2,1)S(1)}, bf16[256,2048]{1,0:T(8,128)(2,1)}, u32[]{:S(2)}) %copy-start) | copy-done | bytes 1048600
  2.5 0.0 copy-start.1
  2.5 0.7 copy-done.1
  3.2 0.0 copy-start.2
  3.2 0.7 copy-done.2
  3.9 0.0 copy-start.3
  3.9 0.7 copy-done.3
  4.6 0.0 copy-start.4
  4.6 0.7 copy-done.4
  5.3 0.0 copy-start.5
  5.3 0.7 copy-done.5
  6.0 0.0 copy-start.6
  6.0 0.7 copy-done.6
  6.6 56.9 %shard_map.119 = (f32[256,512]{1,0:T(8,128)S(1)}, f32[4,256,128]{2,1,0:T(8,128)S(1)}) custom-call(f32[2,512]{1,0:T(2,128)S(1)} %copy-done.3, bf16[2,2048]{1,0:T(2,128)(2,1)S(1)} %copy-done.1, bf16[256,2048]{1,0:T(8,128)(2,1)S(1)} %copy-done, s32[1,512]{1,0:T(1,128)S(1)} %bitcast.1, s32[1,128]{1,0:T(1,128)S(1)} %copy-done.7, s32[16,128]{1,0:T(8,128)S(1)} %copy-done.2, ...), custom_call_target="tpu_custom_call" | custom-call | tf_op jit(solution)/shard_map/pallas_call | solution.py:290
  63.5 6.7 %shard_map.120 = (f32[512,128]{1,0:T(8,128)}, f32[128,128]{1,0:T(8,128)}, f32[64,128]{1,0:T(8,128)}, f32[32,128]{1,0:T(8,128)}, f32[16,256]{1,0:T(8,128)}) custom-call(f32[256,512]{1,0:T(8,128)S(1)} %get-tuple-element.7.sk_ref, f32[4,256,128]{2,1,0:T(8,128)S(1)} %get-tuple-element.8.ch_ref), custom_call_target="tpu_custom_call" | custom-call | tf_op jit(solution)/shard_map/pallas_call | solution.py:325
Async XLA Ops:
  0.6 0.7 copy-start.7
  1.3 1.2 %copy-start = (bf16[256,2048]{1,0:T(8,128)(2,1)S(1)}, bf16[256,2048]{1,0:T(8,128)(2,1)}, u32[]{:S(2)}) copy-start(bf16[256,2048]{1,0:T(8,128)(2,1)} %om_ref.1) | copy-start | bytes 3145732
  2.5 0.7 copy-start.1
  3.2 0.7 copy-start.2
  3.9 0.7 copy-start.3
  4.6 0.7 copy-start.4
  5.3 0.7 copy-start.5
  6.0 0.7 copy-start.6

commit v3 on v2

--- a/solution.py
+++ b/solution.py
@@ -11,7 +11,8 @@
 DELTA_SQUARED = 0.0001
 LEVELS = 3
 LANES = 128
-CHUNK = 256
+CHUNK = 512
+SIDE = 24
 LN2 = 0.6931471805599453
 MESH = pl.DeviceIdType.MESH
 HIGHEST = lax.Precision.HIGHEST
@@ -39,24 +40,48 @@
     return out
 
 
+def flip(value, mask, bits):
+    out = 0
+    for i in range(bits):
+        out = out + (value // 2**i + mask // 2**i) % 2 * 2**i
+    return out
+
+
 def sketch_kernel(
     rows, cols,
-    tgt_ref, src_ref, om_ref, ord_ref, leaf_ref, p1_ref, p2_ref, p3_ref,
-    sk_ref, ch_ref,
-    every, orders, table, src_col, acc, part_out, part_in, z_out, z_in, ex_out, ex_in,
-    tgt_send, tgt_recv, ord_send, ord_recv, part_send, part_recv, z_send, z_recv, ex_send, ex_recv,
+    tgt_hbm, src_hbm, om_hbm, ord_hbm, leaf_hbm, p1_hbm, p2_hbm, p3_hbm,
+    sk_ref, ch_ref, inv_ref,
+    src_ref, om_ref, leaf_ref, p1_ref, p2_ref, p3_ref,
+    every, orders, table, src_left, acc, part_out, part_in, z_out, z_in, ex_out, ex_in,
+    load_sem,
+    tgt_send, tgt_recv, ord_send, ord_recv, part_send, part_recv, z_send, z_recv,
+    ex_send, ex_recv, pass_send, pass_recv,
 ):
     n = rows * cols
     zs = cols // 2
+    bits = zs.bit_length() - 1
     row = lax.axis_index("row")
     col = lax.axis_index("col")
     me = row * cols + col
     z = col // 2
     core = col % 2
     partner = z * 2 + (1 - core)
-    length = ord_ref.shape[1]
-    local = tgt_ref.shape[1]
+    length = ord_hbm.shape[1]
+    local = tgt_hbm.shape[1]
     per = 2 * local // LANES
+
+    loads = [
+        pltpu.make_async_copy(src, dst, load_sem.at[i])
+        for i, (src, dst) in enumerate(
+            (
+                (src_hbm, src_ref), (om_hbm, om_ref), (leaf_hbm, leaf_ref),
+                (p1_hbm, p1_ref), (p2_hbm, p2_ref), (p3_hbm, p3_ref),
+                (tgt_hbm, every.at[me]), (ord_hbm, orders.at[col]),
+            )
+        )
+    ]
+    for load in loads:
+        load.start()
 
     barrier = pltpu.get_barrier_semaphore()
 
@@ -73,7 +98,7 @@
     def tgt_copy(i):
         other = lax.rem(me + i, n)
         return pltpu.make_async_remote_copy(
-            src_ref=tgt_ref, dst_ref=every.at[me],
+            src_ref=tgt_hbm, dst_ref=every.at[me],
             send_sem=tgt_send.at[i], recv_sem=tgt_recv.at[i],
             device_id=(other // cols, other % cols), device_id_type=MESH,
         )
@@ -81,7 +106,7 @@
     def ord_copy(i):
         other = lax.rem(col + i, cols)
         return pltpu.make_async_remote_copy(
-            src_ref=ord_ref, dst_ref=orders.at[col],
+            src_ref=ord_hbm, dst_ref=orders.at[col],
             send_sem=ord_send.at[i], recv_sem=ord_recv.at[i],
             device_id=(row, other), device_id_type=MESH,
         )
@@ -100,10 +125,23 @@
 
     lax.fori_loop(1, n, start(tgt_copy), 0)
     lax.fori_loop(1, cols, start(ord_copy), 0)
-    every[me] = tgt_ref[...]
-    orders[col] = ord_ref[...]
-    wide = src_ref[...].astype(F32)
-    src_col[...] = jnp.concatenate([wide, jnp.zeros((6, wide.shape[1]), F32)], axis=0).T
+    for load in loads:
+        load.wait()
+
+    def pieces(x):
+        return [p.astype(F32) for p in split3(x)]
+
+    wide = src_ref[...].astype(F32) - 0.5
+    sx, sy = wide[0:1], wide[1:2]
+    ones = jnp.ones_like(sx)
+    left = []
+    for part in (-2.0 * sx, -2.0 * sy):
+        a, b, c = pieces(part)
+        left += [a, a, a, b, b, c]
+    left += pieces(sx * sx + sy * sy) + [ones] * 3
+    left += [jnp.zeros_like(sx)] * (SIDE - len(left))
+    src_left[...] = jnp.concatenate(left, axis=0).T.astype(BF16)
+
     lax.fori_loop(1, n, finish(tgt_copy), 0)
     lax.fori_loop(1, cols, finish(ord_copy), 0)
 
@@ -137,72 +175,109 @@
 
     def block(leaf):
         px, py = points_of(leaf)
+        px, py = px - 0.5, py - 0.5
+        right = []
+        for part in (px, py):
+            a, b, c = pieces(part)
+            right += [a, b, c, a, b, a]
+        right += [jnp.ones_like(px)] * 3 + pieces(px * px + py * py + DELTA_SQUARED)
+        right += [jnp.zeros_like(px)] * (SIDE - len(right))
+        points = jnp.concatenate(right, axis=0).astype(BF16)
+
+        def squares(at):
+            return jnp.dot(
+                src_left[at : at + CHUNK, :], points, preferred_element_type=F32
+            )
+
         total = None
+        ahead = squares(0)
         for at in range(0, sources, CHUNK):
-            s = src_col[at : at + CHUNK, :]
-            dx = px - s[:, 0:1]
-            dy = py - s[:, 1:2]
-            panel = (-0.5 * LN2) * jnp.log2(dx * dx + dy * dy + DELTA_SQUARED)
+            now = ahead
+            if at + CHUNK < sources:
+                ahead = squares(at + CHUNK)
+            panel = ((-0.5 * LN2) * jnp.log2(now)).astype(BF16)
             term = jnp.dot(
-                om_ref[:, at : at + CHUNK], panel.astype(BF16), preferred_element_type=F32
+                om_ref[:, at : at + CHUNK], panel, preferred_element_type=F32
             )
             total = term if total is None else total + term
         acc[...] = total
 
-    def part_copy(k):
+    def part_copy(x):
         return pltpu.make_async_remote_copy(
-            src_ref=part_out.at[k], dst_ref=part_in.at[k],
-            send_sem=part_send.at[k], recv_sem=part_recv.at[k],
+            src_ref=part_out.at[x], dst_ref=part_in.at[x],
+            send_sem=part_send.at[x], recv_sem=part_recv.at[x],
             device_id=(row, partner), device_id_type=MESH,
         )
 
-    def z_copy(k):
-        to = lax.rem(z + k, zs)
+    def z_copy(x, b):
         return pltpu.make_async_remote_copy(
-            src_ref=z_out.at[k], dst_ref=z_in.at[k],
-            send_sem=z_send.at[k], recv_sem=z_recv.at[k],
-            device_id=(row, to * 2 + core), device_id_type=MESH,
-        )
-
-    def both(k):
-        to = lax.rem(z + k, zs)
+            src_ref=z_out.at[x], dst_ref=z_in.at[x],
+            send_sem=z_send.at[x], recv_sem=z_recv.at[x],
+            device_id=(row, flip(z, 2**b, bits) * 2 + core), device_id_type=MESH,
+        )
+
+    def both(x, received):
+        to = flip(z, x, bits)
         block(to * 2 + (1 - core))
-        part_out[k] = acc[...].astype(BF16)
-        part_copy(k).start()
+        part_out[x] = acc[...]
+        part_copy(x).start()
         block(to * 2 + core)
-        part_copy(k).wait()
-
-    def step(k, carry):
-        both(k)
-        z_out[k] = (acc[...] + part_in[k].astype(F32)).astype(BF16)
-        z_copy(k).start()
-        return carry
-
-    lax.fori_loop(1, zs, step, 0)
-    both(0)
-    acc[...] += part_in[0].astype(F32)
-
-    def collect(k, carry):
-        z_copy(k).wait()
-        acc[...] += z_in[k].astype(F32)
-        return carry
-
-    lax.fori_loop(1, zs, collect, 0)
-
-    sk_ref[...] = acc[...]
-    chosen = pick_columns(split3(acc[...]), leaf_ref[...])
+        part_copy(x).wait()
+        total = acc[...] + part_in[x]
+        for b in range(received):
+            z_copy(x + 2**b, b).wait()
+            total = total + z_in[x + 2**b].astype(F32)
+        return total
+
+    for b in range(bits):
+        count = zs // 2 ** (b + 1)
+
+        def stage(j, carry, b=b, count=count):
+            x = (2 * (count - 1 - j) + 1) * 2**b
+            z_out[x] = both(x, b).astype(BF16)
+            z_copy(x, b).start()
+            return carry
+
+        lax.fori_loop(0, count, stage, 0)
+    sketch = both(0, bits)
+    sk_ref[...] = sketch
+    chosen = pick_columns(split3(sketch), leaf_ref[...])
     ch_ref[0] = chosen
+    half = chosen.shape[0] // 2
+    mine = pl.ds(pl.multiple_of(core * half, half), half)
     for s, p_ref in enumerate((p1_ref, p2_ref, p3_ref)):
         bit = col // 2**s % 2
         other = col + (1 - 2 * bit) * 2**s
         ex_out[s] = chosen
-        copy = pltpu.make_async_remote_copy(
-            src_ref=ex_out.at[s], dst_ref=ex_in.at[s],
-            send_sem=ex_send.at[s], recv_sem=ex_recv.at[s],
-            device_id=(row, other), device_id_type=MESH,
-        )
-        copy.start()
+        if s == 0:
+            copy = pltpu.make_async_remote_copy(
+                src_ref=ex_out.at[s], dst_ref=ex_in.at[s],
+                send_sem=ex_send.at[s], recv_sem=ex_recv.at[s],
+                device_id=(row, other), device_id_type=MESH,
+            )
+            copy.start()
+        else:
+            copy = pltpu.make_async_remote_copy(
+                src_ref=ex_out.at[s, mine], dst_ref=ex_in.at[s, mine],
+                send_sem=ex_send.at[s], recv_sem=ex_recv.at[s],
+                device_id=(row, other), device_id_type=MESH,
+            )
+            copy.start()
+        if s == LEVELS - 1:
+            inverse = shifted_inverses(
+                [contract0(ch_ref[m], ch_ref[m]) for m in range(LEVELS)]
+            )
+            for m in range(LEVELS):
+                inv_ref[m] = inverse[m]
         copy.wait()
+        if s > 0:
+            relay = pltpu.make_async_remote_copy(
+                src_ref=ex_in.at[s, mine], dst_ref=ex_in.at[s, mine],
+                send_sem=pass_send.at[s], recv_sem=pass_recv.at[s],
+                device_id=(row, partner), device_id_type=MESH,
+            )
+            relay.start()
+            relay.wait()
         theirs = ex_in[s]
         high = bit == 1
         low_part = jnp.where(high, theirs, chosen)
@@ -263,10 +338,11 @@
     return [x / t for x, t in zip(xs, tops)]
 
 
-def solve_kernel(sk_ref, ch_ref, o0, o1, o2, o3, root, r_ref, t_ref):
+def solve_kernel(sk_ref, ch_ref, inv_ref, o0, o1, o2, o3, root, r_ref, t_ref):
     col = lax.axis_index("col")
     levels = ch_ref.shape[0]
-    inverse = shifted_inverses([contract0(ch_ref[m], ch_ref[m]) for m in range(levels)])
+    top = ch_ref[levels - 1]
+    inverse = [inv_ref[m] for m in range(levels - 1)] + shifted_inverses([contract0(top, top)])
     o0[...] = product6(contract0(sk_ref[...], ch_ref[0]), inverse[0])
     for s, o in enumerate((o1, o2, o3)):
         r_ref[...] = contract0(ch_ref[s], ch_ref[s + 1])
@@ -286,54 +362,52 @@
     k = leaf_pivots.shape[1]
     per = targets.size // LANES
     vmem = pl.BlockSpec(memory_space=pltpu.VMEM)
+    hbm = pl.BlockSpec(memory_space=pltpu.HBM)
     dma = lambda *d: pltpu.SemaphoreType.DMA(d)
-    sketch, chosen = pl.pallas_call(
+    held = lambda a: pltpu.VMEM(a.shape, a.dtype)
+    sketch, chosen, inverse = pl.pallas_call(
         functools.partial(sketch_kernel, rows, cols),
         out_shape=(
             jax.ShapeDtypeStruct((width, leaf), F32),
             jax.ShapeDtypeStruct((LEVELS + 1, width, k), F32),
+            jax.ShapeDtypeStruct((LEVELS, k, k), F32),
         ),
-        in_specs=[vmem] * 8,
-        out_specs=(vmem, vmem),
+        in_specs=[hbm] * 8,
+        out_specs=(vmem,) * 3,
         scratch_shapes=[
-            pltpu.VMEM((n, 2, leaf), F32),
+            held(sources), held(omega), held(leaf_pivots), held(p1), held(p2), held(p3),
+            pltpu.VMEM((n, 2, targets.shape[1]), F32),
             pltpu.VMEM((cols, 1, leaf), jnp.int32),
             pltpu.VMEM((3, LANES, n * per), BF16),
-            pltpu.VMEM((sources.shape[1], 8), F32),
+            pltpu.VMEM((sources.shape[1], SIDE), BF16),
             pltpu.VMEM((width, leaf), F32),
-            pltpu.VMEM((zs, width, leaf), BF16),
-            pltpu.VMEM((zs, width, leaf), BF16),
+            pltpu.VMEM((zs, width, leaf), F32),
+            pltpu.VMEM((zs, width, leaf), F32),
             pltpu.VMEM((zs, width, leaf), BF16),
             pltpu.VMEM((zs, width, leaf), BF16),
             pltpu.VMEM((LEVELS, width, k), F32),
             pltpu.VMEM((LEVELS, width, k), F32),
+            dma(8),
             dma(n), dma(n), dma(cols), dma(cols), dma(zs), dma(zs), dma(zs), dma(zs),
-            dma(LEVELS), dma(LEVELS),
+            dma(LEVELS), dma(LEVELS), dma(LEVELS), dma(LEVELS),
         ],
         compiler_params=pltpu.CompilerParams(
-            collective_id=0, has_side_effects=True, vmem_limit_bytes=48 << 20
+            collective_id=0, has_side_effects=True, vmem_limit_bytes=56 << 20
         ),
-    )(
-        targets,
-        sources,
-        omega,
-        tree_order.reshape(1, leaf),
-        leaf_pivots,
-        p1, p2, p3,
-    )
+    )(targets, sources, omega, tree_order.reshape(1, leaf), leaf_pivots, p1, p2, p3)
     out_rows = [leaf] + [k // 2**s for s in range(LEVELS)]
     return pl.pallas_call(
         solve_kernel,
         out_shape=tuple(jax.ShapeDtypeStruct((r, k), F32) for r in out_rows)
         + (jax.ShapeDtypeStruct((k // 2**LEVELS, width), F32),),
-        in_specs=[vmem, vmem],
+        in_specs=[vmem] * 3,
         out_specs=(vmem,) * (len(out_rows) + 1),
         scratch_shapes=[
             pltpu.VMEM((k, k), F32),
             pltpu.VMEM((k, width), F32),
         ],
         compiler_params=pltpu.CompilerParams(vmem_limit_bytes=32 << 20),
-    )(sketch, chosen)
+    )(sketch, chosen, inverse)
 
 
 def solution(mesh):

time: 70.6 us -> 61.1 us (0.87)
  Pallas kernels: 63.6 us -> 57.2 us
  local copies, waits for them, and re-layouts: 6 us -> 3 us
    pallas_call x1, Pallas kernels: 56.9 us -> 51.1 us  [body(): pl.pallas_call(functools.partial(sketch_kernel, rows, cols), out_shape=(j...]
    unnamed x16 -> x6, local copies, waits for them, and re-layouts: 6 us -> 3 us
where the time goes in v3:
time: 61.1 us; the launch traced here: 60.9 us
  Pallas kernels  57.2 us (94%)
  local copies, waits for them, and re-layouts  3 us (5%)
  between operations  0.65 us (1%)
    pallas_call x1, Pallas kernels, body(): pl.pallas_call(functools.partial(sketch_kernel, rows, cols), out_shape=(j...  51.1 us
    pallas_call x1, Pallas kernels, body(): pl.pallas_call(solve_kernel, out_shape=tuple((jax.ShapeDtypeStruct((r, k)...  6.16 us
    unnamed x6, local copies, waits for them, and re-layouts  3 us

profile of v3, /device:TPU:0, one launch (start us, length us, event | category | flops | bytes accessed | tf_op | source)
XLA Modules:
  0.0 60.9 jit_solution(8700679245545659185)
XLA Ops:
  0.6 51.1 %shard_map.119 = (f32[256,512]{1,0:T(8,128)}, f32[4,256,128]{2,1,0:T(8,128)}, f32[3,128,128]{2,1,0:T(8,128)}) custom-call(f32[2,512]{1,0:T(2,128)} %tgt_hbm.1, bf16[2,2048]{1,0:T(2,128)(2,1)} %src_hbm.1, bf16[256,2048]{1,0:T(8,128)(2,1)} %om_hbm.1, s32[1,512]{1,0:T(1,128)} %bitcast.1, s32[1,128]{1,0:T(1,128)} %leaf_hbm.1, s32[16,128]{1,0:T(8,128)} %p1_hbm.1, ...), custom_call_target="tpu_custom_call" | custom-call | tf_op jit(solution)/shard_map/pallas_call | solution.py:368
  51.7 0.0 copy-start
  51.7 1.0 %copy-done = f32[256,512]{1,0:T(8,128)S(1)} copy-done((f32[256,512]{1,0:T(8,128)S(1)}, f32[256,512]{1,0:T(8,128)}, u32[]{:S(2)}) %copy-start) | copy-done | bytes 524312
  52.8 0.0 copy-start.1
  52.8 1.0 %copy-done.1 = f32[4,256,128]{2,1,0:T(8,128)S(1)} copy-done((f32[4,256,128]{2,1,0:T(8,128)S(1)}, f32[4,256,128]{2,1,0:T(8,128)}, u32[]{:S(2)}) %copy-start.1) | copy-done | bytes 524312
  53.8 0.0 copy-start.2
  53.8 0.9 %copy-done.2 = f32[3,128,128]{2,1,0:T(8,128)S(1)} copy-done((f32[3,128,128]{2,1,0:T(8,128)S(1)}, f32[3,128,128]{2,1,0:T(8,128)}, u32[]{:S(2)}) %copy-start.2) | copy-done | bytes 196632
  54.7 6.2 %shard_map.120 = (f32[512,128]{1,0:T(8,128)}, f32[128,128]{1,0:T(8,128)}, f32[64,128]{1,0:T(8,128)}, f32[32,128]{1,0:T(8,128)}, f32[16,256]{1,0:T(8,128)}) custom-call(f32[256,512]{1,0:T(8,128)S(1)} %copy-done, f32[4,256,128]{2,1,0:T(8,128)S(1)} %copy-done.1, f32[3,128,128]{2,1,0:T(8,128)S(1)} %copy-done.2), custom_call_target="tpu_custom_call" | custom-call | tf_op jit(solution)/shard_map/pallas_call | solution.py:399
Async XLA Ops:
  51.7 1.0 %copy-start = (f32[256,512]{1,0:T(8,128)S(1)}, f32[256,512]{1,0:T(8,128)}, u32[]{:S(2)}) copy-start(f32[256,512]{1,0:T(8,128)} %get-tuple-element.8.sk_ref) | copy-start | bytes 1572868
  52.8 1.0 %copy-start.1 = (f32[4,256,128]{2,1,0:T(8,128)S(1)}, f32[4,256,128]{2,1,0:T(8,128)}, u32[]{:S(2)}) copy-start(f32[4,256,128]{2,1,0:T(8,128)} %get-tuple-element.9.ch_ref) | copy-start | bytes 1572868
  53.8 0.9 %copy-start.2 = (f32[3,128,128]{2,1,0:T(8,128)S(1)}, f32[3,128,128]{2,1,0:T(8,128)}, u32[]{:S(2)}) copy-start(f32[3,128,128]{2,1,0:T(8,128)} %get-tuple-element.10.inv_ref) | copy-start | bytes 589828

commit v4 on v3

--- a/solution.py
+++ b/solution.py
@@ -50,7 +50,7 @@
 def sketch_kernel(
     rows, cols,
     tgt_hbm, src_hbm, om_hbm, ord_hbm, leaf_hbm, p1_hbm, p2_hbm, p3_hbm,
-    sk_ref, ch_ref, inv_ref,
+    sk_hbm, ch_ref, inv_ref,
     src_ref, om_ref, leaf_ref, p1_ref, p2_ref, p3_ref,
     every, orders, table, src_left, acc, part_out, part_in, z_out, z_in, ex_out, ex_in,
     load_sem,
@@ -240,7 +240,9 @@
 
         lax.fori_loop(0, count, stage, 0)
     sketch = both(0, bits)
-    sk_ref[...] = sketch
+    acc[...] = sketch
+    keep = pltpu.make_async_copy(acc, sk_hbm, load_sem.at[0])
+    keep.start()
     chosen = pick_columns(split3(sketch), leaf_ref[...])
     ch_ref[0] = chosen
     half = chosen.shape[0] // 2
@@ -285,6 +287,7 @@
         cand = jnp.concatenate([low_part, high_part], axis=1)
         chosen = pick_columns(split3(cand), p_ref[pl.ds(me // 2 ** (s + 1), 1), :])
         ch_ref[s + 1] = chosen
+    keep.wait()
 
 
 def contract0(a, b):
@@ -338,7 +341,19 @@
     return [x / t for x, t in zip(xs, tops)]
 
 
-def solve_kernel(sk_ref, ch_ref, inv_ref, o0, o1, o2, o3, root, r_ref, t_ref):
+def solve_kernel(
+    sk_hbm, ch_hbm, inv_hbm, o0, o1, o2, o3, root, sk_ref, ch_ref, inv_ref, r_ref, t_ref, sem
+):
+    loads = [
+        pltpu.make_async_copy(src, dst, sem.at[i])
+        for i, (src, dst) in enumerate(
+            ((ch_hbm, ch_ref), (sk_hbm, sk_ref), (inv_hbm, inv_ref))
+        )
+    ]
+    for load in loads:
+        load.start()
+    for load in loads:
+        load.wait()
     col = lax.axis_index("col")
     levels = ch_ref.shape[0]
     top = ch_ref[levels - 1]
@@ -373,7 +388,7 @@
             jax.ShapeDtypeStruct((LEVELS, k, k), F32),
         ),
         in_specs=[hbm] * 8,
-        out_specs=(vmem,) * 3,
+        out_specs=(hbm, vmem, vmem),
         scratch_shapes=[
             held(sources), held(omega), held(leaf_pivots), held(p1), held(p2), held(p3),
             pltpu.VMEM((n, 2, targets.shape[1]), F32),
@@ -400,11 +415,13 @@
         solve_kernel,
         out_shape=tuple(jax.ShapeDtypeStruct((r, k), F32) for r in out_rows)
         + (jax.ShapeDtypeStruct((k // 2**LEVELS, width), F32),),
-        in_specs=[vmem] * 3,
+        in_specs=[hbm] * 3,
         out_specs=(vmem,) * (len(out_rows) + 1),
         scratch_shapes=[
+            held(sketch), held(chosen), held(inverse),
             pltpu.VMEM((k, k), F32),
             pltpu.VMEM((k, width), F32),
+            dma(3),
         ],
         compiler_params=pltpu.CompilerParams(vmem_limit_bytes=32 << 20),
     )(sketch, chosen, inverse)

time: 61.1 us -> 61.9 us (1.013)
  no operation moved by 1% of the time
where the time goes in v4:
time: 61.9 us; the launch traced here: 61.6 us
  Pallas kernels  57.8 us (93%)
  local copies, waits for them, and re-layouts  3 us (5%)
  between operations  0.83 us (1%)
    pallas_call x1, Pallas kernels, body(): pl.pallas_call(functools.partial(sketch_kernel, rows, cols), out_shape=(j...  51.1 us
    pallas_call x1, Pallas kernels, body(): pl.pallas_call(solve_kernel, out_shape=tuple((jax.ShapeDtypeStruct((r, k)...  6.72 us
    unnamed x6, local copies, waits for them, and re-layouts  3 us

profile of v4, /device:TPU:0, one launch (start us, length us, event | category | flops | bytes accessed | tf_op | source)
XLA Modules:
  0.0 61.6 jit_solution(14253854436516437709)
XLA Ops:
  0.6 51.1 %shard_map.119 = (f32[256,512]{1,0:T(8,128)}, f32[4,256,128]{2,1,0:T(8,128)}, f32[3,128,128]{2,1,0:T(8,128)}) custom-call(f32[2,512]{1,0:T(2,128)} %tgt_hbm.1, bf16[2,2048]{1,0:T(2,128)(2,1)} %src_hbm.1, bf16[256,2048]{1,0:T(8,128)(2,1)} %om_hbm.1, s32[1,512]{1,0:T(1,128)} %bitcast.1, s32[1,128]{1,0:T(1,128)} %leaf_hbm.1, s32[16,128]{1,0:T(8,128)} %p1_hbm.1, ...), custom_call_target="tpu_custom_call" | custom-call | tf_op jit(solution)/shard_map/pallas_call | solution.py:383
  51.7 0.0 copy-start
  51.7 1.0 %copy-done = f32[256,512]{1,0:T(8,128)S(1)} copy-done((f32[256,512]{1,0:T(8,128)S(1)}, f32[256,512]{1,0:T(8,128)}, u32[]{:S(2)}) %copy-start) | copy-done | bytes 524312
  52.8 0.0 copy-start.1
  52.8 1.0 %copy-done.1 = f32[4,256,128]{2,1,0:T(8,128)S(1)} copy-done((f32[4,256,128]{2,1,0:T(8,128)S(1)}, f32[4,256,128]{2,1,0:T(8,128)}, u32[]{:S(2)}) %copy-start.1) | copy-done | bytes 524312
  53.8 0.0 copy-start.2
  53.8 0.9 %copy-done.2 = f32[3,128,128]{2,1,0:T(8,128)S(1)} copy-done((f32[3,128,128]{2,1,0:T(8,128)S(1)}, f32[3,128,128]{2,1,0:T(8,128)}, u32[]{:S(2)}) %copy-start.2) | copy-done | bytes 196632
  54.7 6.7 %shard_map.120 = (f32[512,128]{1,0:T(8,128)}, f32[128,128]{1,0:T(8,128)}, f32[64,128]{1,0:T(8,128)}, f32[32,128]{1,0:T(8,128)}, f32[16,256]{1,0:T(8,128)}) custom-call(f32[256,512]{1,0:T(8,128)S(1)} %copy-done, f32[4,256,128]{2,1,0:T(8,128)S(1)} %copy-done.1, f32[3,128,128]{2,1,0:T(8,128)S(1)} %copy-done.2), custom_call_target="tpu_custom_call" | custom-call | tf_op jit(solution)/shard_map/pallas_call | solution.py:414
Async XLA Ops:
  51.7 1.0 %copy-start = (f32[256,512]{1,0:T(8,128)S(1)}, f32[256,512]{1,0:T(8,128)}, u32[]{:S(2)}) copy-start(f32[256,512]{1,0:T(8,128)} %get-tuple-element.8.sk_hbm) | copy-start | bytes 1572868
  52.8 1.0 %copy-start.1 = (f32[4,256,128]{2,1,0:T(8,128)S(1)}, f32[4,256,128]{2,1,0:T(8,128)}, u32[]{:S(2)}) copy-start(f32[4,256,128]{2,1,0:T(8,128)} %get-tuple-element.9.ch_hbm) | copy-start | bytes 1572868
  53.8 0.9 %copy-start.2 = (f32[3,128,128]{2,1,0:T(8,128)S(1)}, f32[3,128,128]{2,1,0:T(8,128)}, u32[]{:S(2)}) copy-start(f32[3,128,128]{2,1,0:T(8,128)} %get-tuple-element.10.inv_hbm) | copy-start | bytes 589828
